TPU v7x, 256 devices: a whole 4x4x8 slice. The times are simulated.
256 devices in a mesh: seq: 32 (over z, x_hi, core), fsdp: 8 (over y, x_lo).
Axes of the slice: x: 4 (x_hi: 2, x_lo: 2; x = x_hi * 2 + x_lo), y: 4, z: 8, core: 2. Of those that a mesh axis runs over, the one named last changes fastest.
Arguments:
- queries: bfloat16 [8, 4096, 2048], P('fsdp', 'seq'), may hold values from -6 to 6
- key_vectors: bfloat16 [8, 4096, 2048], P('fsdp', 'seq'), may hold values from -6 to 6
- value_vectors: bfloat16 [8, 4096, 2048], P('fsdp', 'seq'), may hold values from -6 to 6
- out_grad: bfloat16 [8, 4096, 2048], P('fsdp', 'seq'), may hold values from -6 to 6
- out_weight: bfloat16 [2048, 2048], P(None, 'fsdp'), may hold values from -0.125 to 0.125
Outputs:
- query_grad: bfloat16 [8, 4096, 2048], P('fsdp', 'seq')
- key_grad: bfloat16 [8, 4096, 2048], P('fsdp', 'seq')
- value_grad: bfloat16 [8, 4096, 2048], P('fsdp', 'seq')
- weight_grad: float32 [2048, 2048], P('seq', 'fsdp')
All inputs are finite; a program needn't handle non-finite values.
Results may differ from a plain program's by a relative error of at most 0.005.
Values may be sent and summed in bfloat16 or wider, within the bound.
A program may use at most 192 MiB of HBM per device.

v0:
```python
import math
import jax
import jax.numpy as jnp
from jax import lax
from jax.sharding import PartitionSpec as P

HEADS = 16
HEAD_DIM = 128
BLOCK = 128


def carried_in(value, axis, combine, identity, reverse):
    length, here = (lax.axis_size(axis), lax.axis_index(axis))
    everything = lax.all_gather(value, axis)
    start = jnp.broadcast_to(jnp.asarray(identity, value.dtype), value.shape)

    def lap(k, before):
        at = length - 1 - k if reverse else k
        reached = at > here if reverse else at < here
        new = combine(before, everything[at])
        return jnp.where(reached, new, before)

    return lax.fori_loop(0, length, lap, start)


def add_states(earlier, after_dev):
    return earlier + after_dev


def attend(queries, key_vectors, value_vectors, grads, factor):
    batches, tokens, head_count, head_width = queries.shape
    blocks = tokens // BLOCK
    shape_five = (batches, blocks, BLOCK, head_count, head_width)
    query_wide = queries.reshape(shape_five)
    keys_wide = key_vectors.reshape(shape_five)
    values_wide = value_vectors.reshape(shape_five)
    grads_wide = grads.reshape(shape_five)
    single = jnp.float32
    higher = lax.Precision.HIGH
    key_value = jnp.einsum(
        "bnshd,bnshe->bnhde", keys_wide, values_wide, preferred_element_type=single
    )
    query_cot = jnp.einsum(
        "bnthd,bnthe->bnhde", query_wide, grads_wide, preferred_element_type=single
    )
    key_value_dev = jnp.sum(key_value, 1)
    query_cot_dev = jnp.sum(query_cot, 1)
    nothing = jnp.zeros_like(key_value_dev)
    earlier = carried_in(key_value_dev, "seq", add_states, nothing, False)
    after_dev = carried_in(query_cot_dev, "seq", add_states, nothing, True)
    s_before = earlier[:, None] + jnp.cumsum(key_value, 1) - key_value
    g_after = after_dev[:, None] + query_cot_dev[:, None] - jnp.cumsum(query_cot, 1)
    row_index = lax.broadcasted_iota(jnp.int32, (BLOCK, BLOCK), 0)
    col_index = lax.broadcasted_iota(jnp.int32, (BLOCK, BLOCK), 1)
    causal = (row_index >= col_index).astype(jnp.float32)
    scores = jnp.einsum("bnthd,bnshd->bnhts", query_wide, keys_wide, preferred_element_type=single)
    scores = (scores * causal).astype(jnp.bfloat16)
    mixing = jnp.einsum(
        "bnthe,bnshe->bnhts", grads_wide, values_wide, preferred_element_type=single
    )
    mixing = (mixing * causal).astype(jnp.bfloat16)
    attended = jnp.einsum(
        "bnthd,bnhde->bnthe", query_wide.astype(single), s_before, precision=higher
    )
    attended = attended + jnp.einsum(
        "bnhts,bnshe->bnthe", scores, values_wide, preferred_element_type=single
    )
    query_grad = jnp.einsum(
        "bnthe,bnhde->bnthd", grads_wide.astype(single), s_before, precision=higher
    )
    query_grad = query_grad + jnp.einsum(
        "bnhts,bnshd->bnthd", mixing, keys_wide, preferred_element_type=single
    )
    key_grad = jnp.einsum(
        "bnshe,bnhde->bnshd", values_wide.astype(single), g_after, precision=higher
    )
    key_grad = key_grad + jnp.einsum(
        "bnhts,bnthd->bnshd", mixing, query_wide, preferred_element_type=single
    )
    value_grad = jnp.einsum(
        "bnshd,bnhde->bnshe", keys_wide.astype(single), g_after, precision=higher
    )
    value_grad = value_grad + jnp.einsum(
        "bnhts,bnthe->bnshe", scores, grads_wide, preferred_element_type=single
    )
    flat = (batches, tokens, head_count * head_width)
    return (
        factor * attended.reshape(flat),
        factor * query_grad.reshape(flat),
        factor * key_grad.reshape(flat),
        factor * value_grad.reshape(flat),
    )


def split_heads(values_in, head_count):
    return values_in.reshape(values_in.shape[0], values_in.shape[1], head_count, HEAD_DIM)


def body(queries, key_vectors, value_vectors, out_grad, out_weight):
    seq_devices = lax.axis_size("seq")
    fsdp_devices = lax.axis_size("fsdp")
    tokens = queries.shape[1]
    factor = 1.0 / math.sqrt(HEAD_DIM * tokens * seq_devices)
    grad_factor = 1.0 / math.sqrt(fsdp_devices * tokens * seq_devices)
    group_count = HEADS // fsdp_devices
    grads_all = lax.all_gather(out_grad, "fsdp", axis=0, tiled=True)
    grad_attn = jnp.einsum(
        "btd,dc->btc", grads_all, out_weight, preferred_element_type=jnp.float32
    ).astype(jnp.bfloat16)
    moved = (
        lax.all_to_all(queries, "fsdp", split_axis=2, concat_axis=0, tiled=True),
        lax.all_to_all(key_vectors, "fsdp", split_axis=2, concat_axis=0, tiled=True),
        lax.all_to_all(value_vectors, "fsdp", split_axis=2, concat_axis=0, tiled=True),
    )
    attended, query_grad, key_grad, value_grad = attend(
        split_heads(moved[0], group_count),
        split_heads(moved[1], group_count),
        split_heads(moved[2], group_count),
        split_heads(grad_attn, group_count),
        factor,
    )
    returned = (
        lax.all_to_all(
            query_grad.astype(jnp.bfloat16), "fsdp", split_axis=0, concat_axis=2, tiled=True
        ),
        lax.all_to_all(
            key_grad.astype(jnp.bfloat16), "fsdp", split_axis=0, concat_axis=2, tiled=True
        ),
        lax.all_to_all(
            value_grad.astype(jnp.bfloat16), "fsdp", split_axis=0, concat_axis=2, tiled=True
        ),
    )
    attended_low = attended.astype(jnp.bfloat16)
    weight_grad = (
        lax.psum_scatter(
            lax.dot_general(
                grads_all,
                attended_low,
                (((0, 1), (0, 1)), ((), ())),
                preferred_element_type=jnp.float32,
            ),
            "seq",
            scatter_dimension=0,
            tiled=True,
        )
        * grad_factor
    )
    return (returned[0], returned[1], returned[2], weight_grad)


def solution(mesh):
    in_specs = (
        P("fsdp", "seq", None),
        P("fsdp", "seq", None),
        P("fsdp", "seq", None),
        P("fsdp", "seq", None),
        P(None, "fsdp"),
    )
    out_specs = (
        P("fsdp", "seq", None),
        P("fsdp", "seq", None),
        P("fsdp", "seq", None),
        P("seq", "fsdp"),
    )
    return jax.shard_map(body, mesh=mesh, in_specs=in_specs, out_specs=out_specs, check_vma=False)
```

profile of v0, /device:TPU:8, one launch (start us, length us, event | category | flops | bytes accessed | tf_op | source)
XLA Modules:
  0.0 716.8 jit_solution(7374934269452240862)
XLA Ops:
  7.9 2.4 copy.72
  10.8 11.5 %reduce = bf16[2048,128]{1,0:T(8,128)(2,1)S(1)} reduce(bf16[2048,1,128]{2,1,0:T(2,128)(2,1)S(1)} %bitcast.143, bf16[]{:T(256)} %broadcast.48), dimensions={1}, to_apply=%bitcast.91.reduce_sub_computation | reduce | bytes 1048578
  23.2 5.8 all-to-all-start
  29.1 2.3 copy.73
  31.4 11.5 %reduce.1 = bf16[2048,128]{1,0:T(8,128)(2,1)S(1)} reduce(bf16[2048,1,128]{2,1,0:T(2,128)(2,1)S(1)} %bitcast.145, bf16[]{:T(256)} %broadcast.48), dimensions={1}, to_apply=%bitcast.93.reduce_sub_computation | reduce | bytes 1048578
  43.9 5.9 all-to-all-start.1
  50.4 13.2 %all-to-all-done.1 = bf16[8,2,16384]{2,1,0:T(2,128)(2,1)} async-done(((bf16[8,2,16384]{2,1,0:T(2,128)(2,1)}), bf16[8,2,16384]{2,1,0:T(2,128)(2,1)}, u32[]{:S(2)}, u32[]{:S(2)}) %all-to-all-start.1) | async-done | bytes 524320 | tf_op jit(solution)/shard_map/all_to_all | solution.py:113
  63.7 2.2 reshape.158
  69.2 11.5 %reduce.2 = bf16[2048,128]{1,0:T(8,128)(2,1)S(1)} reduce(bf16[2048,1,128]{2,1,0:T(2,128)(2,1)S(1)} %bitcast.144, bf16[]{:T(256)} %broadcast.48), dimensions={1}, to_apply=%bitcast.95.reduce_sub_computation | reduce | bytes 1048578
  80.9 18.6 %all_to_all.99 = bf16[8,2,16384]{2,1,0:T(2,128)(2,1)S(1)} all-to-all(bf16[8,2,16384]{2,1,0:T(2,128)(2,1)S(1)} %reshape.159), channel_id=1, replica_groups=mesh['seq'=32,'fsdp'=8] {'fsdp'}, dimensions={0} | all-to-all | bytes 1048576 | tf_op jit(solution)/shard_map/all_to_all | solution.py:111
  100.2 21.6 %all-gather.6.cloned.1.call-done = bf16[8,128,2048]{2,1,0:T(8,128)(2,1)} async-done(((bf16[1,128,2048]{2,1,0:T(8,128)(2,1)}), bf16[8,128,2048]{2,1,0:T(8,128)(2,1)}) %all-gather.6.cloned.1.call-update) | async-done | bytes 4194320 | tf_op jit(solution)/shard_map/all_gather | solution.py:106
  121.7 3.4 convolution_convert_fusion
  127.4 2.3 fusion.12
  129.7 2.3 fusion.11
  132.0 220.7 %all-gather.8.cloned.1.call-done = f32[256,2,128,128]{3,2,1,0:T(8,128)} async-done(((f32[8,2,128,128]{3,2,1,0:T(8,128)}), f32[256,2,128,128]{3,2,1,0:T(8,128)}) %all-gather.8.cloned.1.call-update) | async-done | bytes 33554448 | tf_op jit(solution)/shard_map/all_gather | solution.py:14
  352.8 51.9 %while.30 = (s32[]{:T(128)}, f32[8,2,128,128]{3,2,1,0:T(8,128)S(1)}, s32[]{:T(128)}, f32[32,8,2,128,128]{4,3,2,1,0:T(8,128)}, s32[]{:T(128)}, /*index=5*/s32[]{:T(128)}) while((s32[]{:T(128)}, f32[8,2,128,128]{3,2,1,0:T(8,128)S(1)}, s32[]{:T(128)}, f32[32,8,2,128,128]{4,3,2,1,0:T(8,128)}, s32[]{:T(128)}, /*index=5*/s32[]{:T(128)}) %tuple.92), condition=%wide.region_1.0_spmd.clone, body=%wide.region_0.0_spmd.clone.sunk | while | flops 786436 | bytes 3145821 | solution.py:23
  364.1 1.7 add_select_fusion.4
  365.8 1.6 add_select_fusion.4
  378.8 1.6 add_select_fusion.4
  393.4 1.6 add_select_fusion.4
  395.0 1.6 add_select_fusion.4
  403.1 1.6 add_select_fusion.4
  404.7 2.3 fusion.14
  407.0 1.7 fusion.9
  408.7 2.6 convolution_bitcast_fusion
  411.4 2.9 copy.108
  414.2 1.8 fusion.15
  416.0 2.5 fusion.7
  418.5 5.1 all-to-all-start.2
  424.2 159.7 %all-gather.10.cloned.1.call-done = f32[256,2,128,128]{3,2,1,0:T(8,128)} async-done(((f32[8,2,128,128]{3,2,1,0:T(8,128)}), f32[256,2,128,128]{3,2,1,0:T(8,128)}) %all-gather.10.cloned.1.call-update) | async-done | bytes 33554448 | tf_op jit(solution)/shard_map/all_gather | solution.py:14
  583.9 52.1 %while.31 = (s32[]{:T(128)}, f32[8,2,128,128]{3,2,1,0:T(8,128)S(1)}, s32[]{:T(128)}, f32[32,8,2,128,128]{4,3,2,1,0:T(8,128)}, s32[]{:T(128)}, /*index=5*/s32[]{:T(128)}, s32[]{:T(128)}, s32[]{:T(128)}) while((s32[]{:T(128)}, f32[8,2,128,128]{3,2,1,0:T(8,128)S(1)}, s32[]{:T(128)}, f32[32,8,2,128,128]{4,3,2,1,0:T(8,128)}, s32[]{:T(128)}, ...), condition=%wide.region_3.4_spmd.clone, body=%wide.region_2.3_spmd.clone.sunk | while | flops 786440 | bytes 3145883 | solution.py:23
  583.9 1.6 add_select_fusion.5
  600.2 1.6 add_select_fusion.5
  601.8 1.6 add_select_fusion.5
  606.7 1.6 add_select_fusion.5
  608.4 1.6 add_select_fusion.5
  611.7 1.6 add_select_fusion.5
  613.3 1.6 add_select_fusion.5
  637.4 1.7 fusion.16
  639.1 2.3 fusion.8
  641.5 5.1 all-to-all-start.5
  646.6 2.0 fusion.17
  648.7 2.1 fusion.10
  650.8 4.3 all-to-all-done.5
  655.1 5.5 all-to-all-start.4
  660.6 2.0 copy.105
  662.6 42.9 %reduce-scatter.4.cloned.1.call-done = f32[64,256]{1,0:T(8,128)} async-done(((f32[2048,256]{1,0:T(8,128)}), f32[64,256]{1,0:T(8,128)}) %reduce-scatter.4.cloned.1.call-update) | async-done | bytes 65552
  707.2 2.0 copy.107
  (106 shorter events, 95.7 us)
Async XLA Ops:
  7.2 114.6 %copy-start = (bf16[2048,256]{1,0:T(8,128)(2,1)S(1)}, bf16[2048,256]{1,0:T(8,128)(2,1)}, u32[]{:S(2)}) copy-start(bf16[2048,256]{1,0:T(8,128)(2,1)} %param.13) | copy-start | bytes 3145732
  7.2 114.6 %all-gather.6.cloned.1.call-start = ((), (), s32[]{:S(2)}) async-start(), calls=%async_computation.7 | async-start | bytes 4718592 | tf_op jit(solution)/shard_map/all_gather | solution.py:106
  23.2 20.6 %all-to-all-start = ((bf16[8,2,16384]{2,1,0:T(2,128)(2,1)}), bf16[8,2,16384]{2,1,0:T(2,128)(2,1)S(1)}, u32[]{:S(2)}, u32[]{:S(2)}) async-start(bf16[8,2,16384]{2,1,0:T(2,128)(2,1)} %reshape.155), calls=%async_computation | async-start | bytes 1048576 | tf_op jit(solution)/shard_map/all_to_all | solution.py:112
  43.9 19.8 %all-to-all-start.1 = ((bf16[8,2,16384]{2,1,0:T(2,128)(2,1)}), bf16[8,2,16384]{2,1,0:T(2,128)(2,1)}, u32[]{:S(2)}, u32[]{:S(2)}) async-start(bf16[8,2,16384]{2,1,0:T(2,128)(2,1)} %reshape.157), calls=%async_computation.1 | async-start | bytes 1048576 | tf_op jit(solution)/shard_map/all_to_all | solution.py:113
  49.8 303.0 %all-gather.8.cloned.1.call-start = ((), (), s32[]{:S(2)}) async-start(), calls=%async_computation.8 | async-start | bytes 34603008 | tf_op jit(solution)/shard_map/all_gather | solution.py:14
  50.3 18.1 %copy-start.9 = (bf16[1,128,2048]{2,1,0:T(8,128)(2,1)S(1)}, bf16[1,128,2048]{2,1,0:T(8,128)(2,1)}, u32[]{:S(2)}) copy-start(bf16[1,128,2048]{2,1,0:T(8,128)(2,1)} %param.9) | copy-start | bytes 1572868
  50.4 30.4 %copy-start.4 = (bf16[1,128,2048]{1,2,0:T(8,128)(2,1)}, bf16[1,128,2048]{1,2,0:T(8,128)(2,1)S(1)}, u32[]{:S(2)}) copy-start(bf16[1,128,2048]{1,2,0:T(8,128)(2,1)S(1)} %copy.110) | copy-start | bytes 1572868
  66.0 0.8 copy-start.2
  68.2 515.7 %all-gather.10.cloned.1.call-start = ((), (), s32[]{:S(2)}) async-start(), calls=%async_computation.9 | async-start | bytes 34603008 | tf_op jit(solution)/shard_map/all_gather | solution.py:14
  100.2 25.3 %copy-start.6 = (bf16[1,128,2048]{1,2,0:T(8,128)(2,1)}, bf16[1,128,2048]{1,2,0:T(8,128)(2,1)S(1)}, u32[]{:S(2)}) copy-start(bf16[1,128,2048]{1,2,0:T(8,128)(2,1)S(1)} %copy.112) | copy-start | bytes 1572868
  125.5 1.9 copy-start.8
  404.7 4.0 copy-start.10
  418.5 222.9 %all-to-all-start.2 = ((bf16[8,128,256]{1,2,0:T(8,128)(2,1)}), bf16[8,128,256]{1,2,0:T(8,128)(2,1)}, u32[]{:S(2)}, u32[]{:S(2)}) async-start(bf16[8,128,256]{1,2,0:T(8,128)(2,1)} %bitcast.11), calls=%async_computation.2 | async-start | bytes 1048576 | tf_op jit(solution)/shard_map/all_to_all | solution.py:123
  423.6 281.9 %reduce-scatter.4.cloned.1.call-start = ((), (), s32[]{:S(2)}) async-start(), calls=%async_computation.10 | async-start | bytes 2162688
  583.9 53.5 %copy-start.5 = (bf16[1,128,2048]{1,2,0:T(8,128)(2,1)S(1)}, bf16[1,128,2048]{1,2,0:T(8,128)(2,1)}, u32[]{:S(2)}) copy-start(bf16[1,128,2048]{1,2,0:T(8,128)(2,1)} %copy-done.4) | copy-start | bytes 1572868
  637.4 9.2 %copy-start.3 = (bf16[1,128,2048]{1,2,0:T(8,128)(2,1)S(1)}, bf16[1,128,2048]{1,2,0:T(8,128)(2,1)}, u32[]{:S(2)}) copy-start(bf16[1,128,2048]{1,2,0:T(8,128)(2,1)} %copy-done.2) | copy-start | bytes 1572868
  639.1 9.5 %copy-start.7 = (bf16[1,128,2048]{1,2,0:T(8,128)(2,1)S(1)}, bf16[1,128,2048]{1,2,0:T(8,128)(2,1)}, u32[]{:S(2)}) copy-start(bf16[1,128,2048]{1,2,0:T(8,128)(2,1)} %copy-done.6) | copy-start | bytes 1572868
  641.5 13.6 %all-to-all-start.5 = ((bf16[8,128,256]{1,2,0:T(8,128)(2,1)}), bf16[8,128,256]{1,2,0:T(8,128)(2,1)}, u32[]{:S(2)}, u32[]{:S(2)}) async-start(bf16[8,128,256]{1,2,0:T(8,128)(2,1)} %bitcast.146), calls=%async_computation.5 | async-start | bytes 1048576 | tf_op jit(solution)/shard_map/all_to_all | solution.py:129
  646.6 63.7 %copy-start.1 = (bf16[2048,256]{1,0:T(8,128)(2,1)S(1)}, bf16[2048,256]{1,0:T(8,128)(2,1)}, u32[]{:S(2)}) copy-start(bf16[2048,256]{1,0:T(8,128)(2,1)} %param.13) | copy-start | bytes 3145732
  655.1 54.1 %all-to-all-start.4 = ((bf16[8,128,256]{1,2,0:T(8,128)(2,1)}), bf16[8,128,256]{1,2,0:T(8,128)(2,1)S(1)}, u32[]{:S(2)}, u32[]{:S(2)}) async-start(bf16[8,128,256]{1,2,0:T(8,128)(2,1)} %bitcast.23), calls=%async_computation.4 | async-start | bytes 1048576 | tf_op jit(solution)/shard_map/all_to_all | solution.py:126
Sparse Core Ops, SparseCore 0:
  9.8 111.9 all-gather.5
  124.5 228.2 all-gather.7
  355.6 228.2 all-gather.9
  587.9 117.6 reduce-scatter.3
where the time goes:
time: 720 us; the launch traced here: 717 us
  waiting for transfers between devices  464 us (64%)
  other arithmetic  137 us (19%)
  matrix products  29.2 us (4%)
  starting transfers between devices  27.7 us (4%)
  local copies, waits for them, and re-layouts  24.8 us (3%)
  blocking collectives  18.6 us (3%)
  between operations  14.1 us (2%)
    all_gather x2, waiting for transfers between devices, carried_in(): everything = lax.all_gather(value, axis)  380 us
    select_n x64, other arithmetic, lap(): return jnp.where(reached, new, before)  102 us
    unnamed x5, waiting for transfers between devices  44.2 us
    unnamed x5, other arithmetic  34.6 us
    all_gather x1, waiting for transfers between devices, body(): grads_all = lax.all_gather(out_grad, 'fsdp', axis=0, tiled=True)  21.6 us
    all_to_all x1, blocking collectives, body(): lax.all_to_all(queries, 'fsdp', split_axis=2, concat_axis=0, tiled=True)  18.6 us
    unnamed x38, local copies, waits for them, and re-layouts  16.8 us
  transfers between devices with their start and end apart: 9, of which 6 were waited for; matrix products, arithmetic and copies ran while one was open for 26% of the time, Pallas kernels for 0%

commit v1 on v0

--- a/solution.py
+++ b/solution.py
@@ -103,7 +103,8 @@
     factor = 1.0 / math.sqrt(HEAD_DIM * tokens * seq_devices)
     grad_factor = 1.0 / math.sqrt(fsdp_devices * tokens * seq_devices)
     group_count = HEADS // fsdp_devices
-    grads_all = lax.all_gather(out_grad, "fsdp", axis=0, tiled=True)
+    outgoing = jnp.stack([out_grad] * lax.axis_size("fsdp"))
+    grads_all = jnp.concatenate(lax.all_to_all(outgoing, "fsdp", 0, 0), axis=0)
     grad_attn = jnp.einsum(
         "btd,dc->btc", grads_all, out_weight, preferred_element_type=jnp.float32
     ).astype(jnp.bfloat16)

time: 720 us -> 673 us (0.935)
  waiting for transfers between devices: 464 us -> 404 us
    all_gather x2, waiting for transfers between devices: 380 us -> 294 us  [carried_in(): everything = lax.all_gather(value, axis)]
    all_to_all x0 -> x1, waiting for transfers between devices: none -> 55.7 us  [body(): grads_all = jnp.concatenate(lax.all_to_all(outgoing, 'fsdp', 0, 0), axis=0)]
    all_gather x1 -> x0, waiting for transfers between devices: 21.6 us -> none  [body(): grads_all = lax.all_gather(out_grad, 'fsdp', axis=0, tiled=True)]
    unnamed x5 -> x4, waiting for transfers between devices: 44.2 us -> 42.5 us
    unnamed x38 -> x36, local copies, waits for them, and re-layouts: 16.8 us -> 16.8 us
where the time goes in v1:
time: 673 us; the launch traced here: 669 us
  waiting for transfers between devices  404 us (60%)
  other arithmetic  137 us (20%)
  starting transfers between devices  34.7 us (5%)
  matrix products  31.3 us (5%)
  local copies, waits for them, and re-layouts  28.4 us (4%)
  blocking collectives  17.9 us (3%)
  between operations  14 us (2%)
    all_gather x2, waiting for transfers between devices, carried_in(): everything = lax.all_gather(value, axis)  294 us
    select_n x64, other arithmetic, lap(): return jnp.where(reached, new, before)  103 us
    all_to_all x1, waiting for transfers between devices, body(): grads_all = jnp.concatenate(lax.all_to_all(outgoing, 'fsdp', 0, 0), axis=0)  55.7 us
    unnamed x4, waiting for transfers between devices  42.5 us
    unnamed x5, other arithmetic  34.6 us
    all_to_all x1, blocking collectives, body(): lax.all_to_all(queries, 'fsdp', split_axis=2, concat_axis=0, tiled=True)  17.9 us
    unnamed x36, local copies, waits for them, and re-layouts  16.8 us
  transfers between devices with their start and end apart: 9, of which 6 were waited for; matrix products, arithmetic and copies ran while one was open for 26% of the time, Pallas kernels for 0%

profile of v1, /device:TPU:8, one launch (start us, length us, event | category | flops | bytes accessed | tf_op | source)
XLA Modules:
  0.0 669.4 jit_solution(4301779009085211165)
XLA Ops:
  7.2 2.4 copy.72
  10.1 11.5 %reduce = bf16[2048,128]{1,0:T(8,128)(2,1)S(1)} reduce(bf16[2048,1,128]{2,1,0:T(2,128)(2,1)S(1)} %bitcast.151, bf16[]{:T(256)} %broadcast.51), dimensions={1}, to_apply=%bitcast.101.reduce_sub_computation | reduce | bytes 1048578
  22.6 5.8 all-to-all-start
  28.4 2.3 copy.73
  30.8 11.5 %reduce.1 = bf16[2048,128]{1,0:T(8,128)(2,1)S(1)} reduce(bf16[2048,1,128]{2,1,0:T(2,128)(2,1)S(1)} %bitcast.153, bf16[]{:T(256)} %broadcast.51), dimensions={1}, to_apply=%bitcast.103.reduce_sub_computation | reduce | bytes 1048578
  43.2 5.7 all-to-all-start.1
  49.6 7.1 %all-to-all-done.1 = bf16[8,2,16384]{2,1,0:T(2,128)(2,1)} async-done(((bf16[8,2,16384]{2,1,0:T(2,128)(2,1)}), bf16[8,2,16384]{2,1,0:T(2,128)(2,1)}, u32[]{:S(2)}, u32[]{:S(2)}) %all-to-all-start.1) | async-done | bytes 524320 | tf_op jit(solution)/shard_map/all_to_all | solution.py:114
  56.7 2.2 reshape.163
  62.1 11.5 %reduce.2 = bf16[2048,128]{1,0:T(8,128)(2,1)S(1)} reduce(bf16[2048,1,128]{2,1,0:T(2,128)(2,1)S(1)} %bitcast.152, bf16[]{:T(256)} %broadcast.51), dimensions={1}, to_apply=%bitcast.105.reduce_sub_computation | reduce | bytes 1048578
  73.7 17.9 %all_to_all.104 = bf16[8,2,16384]{2,1,0:T(2,128)(2,1)S(1)} all-to-all(bf16[8,2,16384]{2,1,0:T(2,128)(2,1)S(1)} %reshape.164), channel_id=1, replica_groups=mesh['seq'=32,'fsdp'=8] {'fsdp'}, dimensions={0} | all-to-all | bytes 1048576 | tf_op jit(solution)/shard_map/all_to_all | solution.py:112
  91.6 3.5 stack.2
  95.2 7.1 %all-to-all-start.2 = ((bf16[8,1,128,2048]{3,2,1,0:T(8,128)(2,1)}), bf16[8,1,128,2048]{3,2,1,0:T(8,128)(2,1)}, u32[]{:S(2)}, u32[]{:S(2)}) async-start(bf16[8,1,128,2048]{3,2,1,0:T(8,128)(2,1)} %stack.2), calls=%async_computation.2 | async-start | bytes 8388608 | tf_op jit(solution)/shard_map/all_to_all | solution.py:107
  102.9 55.7 %all-to-all-done.2 = bf16[8,1,128,2048]{3,2,1,0:T(8,128)(2,1)} async-done(((bf16[8,1,128,2048]{3,2,1,0:T(8,128)(2,1)}), bf16[8,1,128,2048]{3,2,1,0:T(8,128)(2,1)}, u32[]{:S(2)}, u32[]{:S(2)}) %all-to-all-start.2) | async-done | bytes 4194336 | tf_op jit(solution)/shard_map/all_to_all | solution.py:107
  158.6 3.4 fusion.20
  164.2 2.3 fusion.19
  166.5 2.3 fusion.18
  168.9 136.2 %all-gather.5.cloned.1.call-done = f32[256,2,128,128]{3,2,1,0:T(8,128)} async-done(((f32[8,2,128,128]{3,2,1,0:T(8,128)}), f32[256,2,128,128]{3,2,1,0:T(8,128)}) %all-gather.5.cloned.1.call-update) | async-done | bytes 33554448 | tf_op jit(solution)/shard_map/all_gather | solution.py:14
  305.1 51.9 %while.30 = (s32[]{:T(128)}, f32[8,2,128,128]{3,2,1,0:T(8,128)S(1)}, s32[]{:T(128)}, f32[32,8,2,128,128]{4,3,2,1,0:T(8,128)}, s32[]{:T(128)}, /*index=5*/s32[]{:T(128)}) while((s32[]{:T(128)}, f32[8,2,128,128]{3,2,1,0:T(8,128)S(1)}, s32[]{:T(128)}, f32[32,8,2,128,128]{4,3,2,1,0:T(8,128)}, s32[]{:T(128)}, /*index=5*/s32[]{:T(128)}) %tuple.90), condition=%wide.region_1.0_spmd.clone, body=%wide.region_0.0_spmd.clone.sunk | while | flops 786436 | bytes 3145829 | solution.py:23
  316.4 1.7 add_select_fusion.4
  318.1 1.6 add_select_fusion.4
  331.1 1.6 add_select_fusion.4
  334.3 1.6 add_select_fusion.4
  345.6 1.6 add_select_fusion.4
  347.3 1.6 add_select_fusion.4
  355.4 1.6 add_select_fusion.4
  357.0 2.1 fusion.24
  359.1 1.7 fusion.16
  360.8 4.9 fusion.4
  365.7 2.9 copy.108
  368.6 1.8 fusion.25
  370.4 2.5 fusion.14
  372.9 5.7 all-to-all-start.3
  379.4 158.1 %all-gather.7.cloned.1.call-done = f32[256,2,128,128]{3,2,1,0:T(8,128)} async-done(((f32[8,2,128,128]{3,2,1,0:T(8,128)}), f32[256,2,128,128]{3,2,1,0:T(8,128)}) %all-gather.7.cloned.1.call-update) | async-done | bytes 33554448 | tf_op jit(solution)/shard_map/all_gather | solution.py:14
  537.5 52.3 %while.31 = (s32[]{:T(128)}, f32[8,2,128,128]{3,2,1,0:T(8,128)S(1)}, s32[]{:T(128)}, f32[32,8,2,128,128]{4,3,2,1,0:T(8,128)}, s32[]{:T(128)}, /*index=5*/s32[]{:T(128)}, s32[]{:T(128)}, s32[]{:T(128)}) while((s32[]{:T(128)}, f32[8,2,128,128]{3,2,1,0:T(8,128)S(1)}, s32[]{:T(128)}, f32[32,8,2,128,128]{4,3,2,1,0:T(8,128)}, s32[]{:T(128)}, ...), condition=%wide.region_3.4_spmd.clone, body=%wide.region_2.3_spmd.clone.sunk | while | flops 786440 | bytes 3145891 | solution.py:23
  537.5 1.6 add_select_fusion.5
  555.4 1.6 add_select_fusion.5
  558.7 1.6 add_select_fusion.5
  588.0 1.8 add_select_fusion.5
  591.1 2.0 fusion.27
  593.2 2.3 fusion.17
  595.5 4.8 all-to-all-start.5
  600.4 1.8 fusion.26
  602.1 2.1 fusion.15
  604.3 4.6 all-to-all-done.5
  608.9 5.5 all-to-all-start.6
  614.3 2.0 copy.105
  616.4 41.8 %reduce-scatter.4.cloned.1.call-done = f32[64,256]{1,0:T(8,128)} async-done(((f32[2048,256]{1,0:T(8,128)}), f32[64,256]{1,0:T(8,128)}) %reduce-scatter.4.cloned.1.call-update) | async-done | bytes 65552
  659.8 2.0 copy.106
  (104 shorter events, 98.1 us)
Async XLA Ops:
  7.2 151.4 %copy-start = (bf16[2048,256]{1,0:T(8,128)(2,1)S(1)}, bf16[2048,256]{1,0:T(8,128)(2,1)}, u32[]{:S(2)}) copy-start(bf16[2048,256]{1,0:T(8,128)(2,1)} %param.13) | copy-start | bytes 3145732
  22.6 20.6 %all-to-all-start = ((bf16[8,2,16384]{2,1,0:T(2,128)(2,1)}), bf16[8,2,16384]{2,1,0:T(2,128)(2,1)S(1)}, u32[]{:S(2)}, u32[]{:S(2)}) async-start(bf16[8,2,16384]{2,1,0:T(2,128)(2,1)} %reshape.160), calls=%async_computation | async-start | bytes 1048576 | tf_op jit(solution)/shard_map/all_to_all | solution.py:113
  43.2 13.5 %all-to-all-start.1 = ((bf16[8,2,16384]{2,1,0:T(2,128)(2,1)}), bf16[8,2,16384]{2,1,0:T(2,128)(2,1)}, u32[]{:S(2)}, u32[]{:S(2)}) async-start(bf16[8,2,16384]{2,1,0:T(2,128)(2,1)} %reshape.162), calls=%async_computation.1 | async-start | bytes 1048576 | tf_op jit(solution)/shard_map/all_to_all | solution.py:114
  48.9 256.1 %all-gather.5.cloned.1.call-start = ((), (), s32[]{:S(2)}) async-start(), calls=%async_computation.8 | async-start | bytes 34603008 | tf_op jit(solution)/shard_map/all_gather | solution.py:14
  49.5 11.8 %copy-start.9 = (bf16[1,128,2048]{2,1,0:T(8,128)(2,1)S(1)}, bf16[1,128,2048]{2,1,0:T(8,128)(2,1)}, u32[]{:S(2)}) copy-start(bf16[1,128,2048]{2,1,0:T(8,128)(2,1)} %param.9) | copy-start | bytes 1572868
  49.6 24.0 %copy-start.2 = (bf16[1,128,2048]{1,2,0:T(8,128)(2,1)}, bf16[1,128,2048]{1,2,0:T(8,128)(2,1)S(1)}, u32[]{:S(2)}) copy-start(bf16[1,128,2048]{1,2,0:T(8,128)(2,1)S(1)} %copy.110) | copy-start | bytes 1572868
  59.0 0.8 copy-start.4
  95.2 63.4 %all-to-all-start.2 = ((bf16[8,1,128,2048]{3,2,1,0:T(8,128)(2,1)}), bf16[8,1,128,2048]{3,2,1,0:T(8,128)(2,1)}, u32[]{:S(2)}, u32[]{:S(2)}) async-start(bf16[8,1,128,2048]{3,2,1,0:T(8,128)(2,1)} %stack.2), calls=%async_computation.2 | async-start | bytes 8388608 | tf_op jit(solution)/shard_map/all_to_all | solution.py:107
  102.3 435.2 %all-gather.7.cloned.1.call-start = ((), (), s32[]{:S(2)}) async-start(), calls=%async_computation.9 | async-start | bytes 34603008 | tf_op jit(solution)/shard_map/all_gather | solution.py:14
  102.9 59.4 %copy-start.6 = (bf16[1,128,2048]{1,2,0:T(8,128)(2,1)}, bf16[1,128,2048]{1,2,0:T(8,128)(2,1)S(1)}, u32[]{:S(2)}) copy-start(bf16[1,128,2048]{1,2,0:T(8,128)(2,1)S(1)} %copy.112) | copy-start | bytes 1572868
  162.3 1.8 copy-start.7
  372.9 222.6 %all-to-all-start.3 = ((bf16[8,128,256]{1,2,0:T(8,128)(2,1)}), bf16[8,128,256]{1,2,0:T(8,128)(2,1)}, u32[]{:S(2)}, u32[]{:S(2)}) async-start(bf16[8,128,256]{1,2,0:T(8,128)(2,1)} %bitcast.13), calls=%async_computation.3 | async-start | bytes 1048576 | tf_op jit(solution)/shard_map/all_to_all | solution.py:124
  378.7 279.5 %reduce-scatter.4.cloned.1.call-start = ((), (), s32[]{:S(2)}) async-start(), calls=%async_computation.10 | async-start | bytes 2162688
  537.5 53.6 %copy-start.5 = (bf16[1,128,2048]{1,2,0:T(8,128)(2,1)S(1)}, bf16[1,128,2048]{1,2,0:T(8,128)(2,1)}, u32[]{:S(2)}) copy-start(bf16[1,128,2048]{1,2,0:T(8,128)(2,1)} %copy-done.4) | copy-start | bytes 1572868
  591.1 9.2 %copy-start.3 = (bf16[1,128,2048]{1,2,0:T(8,128)(2,1)S(1)}, bf16[1,128,2048]{1,2,0:T(8,128)(2,1)}, u32[]{:S(2)}) copy-start(bf16[1,128,2048]{1,2,0:T(8,128)(2,1)} %copy-done.2) | copy-start | bytes 1572868
  593.2 9.0 %copy-start.8 = (bf16[8,128,256]{1,2,0:T(8,128)(2,1)S(1)}, bf16[8,128,256]{1,2,0:T(8,128)(2,1)}, u32[]{:S(2)}) copy-start(bf16[8,128,256]{1,2,0:T(8,128)(2,1)} %copy-done.7) | copy-start | bytes 1572868
  595.5 13.4 %all-to-all-start.5 = ((bf16[8,128,256]{1,2,0:T(8,128)(2,1)}), bf16[8,128,256]{1,2,0:T(8,128)(2,1)}, u32[]{:S(2)}, u32[]{:S(2)}) async-start(bf16[8,128,256]{1,2,0:T(8,128)(2,1)} %bitcast.154), calls=%async_computation.5 | async-start | bytes 1048576 | tf_op jit(solution)/shard_map/all_to_all | solution.py:127
  600.4 62.5 %copy-start.1 = (bf16[2048,256]{1,0:T(8,128)(2,1)S(1)}, bf16[2048,256]{1,0:T(8,128)(2,1)}, u32[]{:S(2)}) copy-start(bf16[2048,256]{1,0:T(8,128)(2,1)} %param.13) | copy-start | bytes 3145732
  608.9 53.0 %all-to-all-start.6 = ((bf16[8,128,256]{1,2,0:T(8,128)(2,1)}), bf16[8,128,256]{1,2,0:T(8,128)(2,1)S(1)}, u32[]{:S(2)}, u32[]{:S(2)}) async-start(bf16[8,128,256]{1,2,0:T(8,128)(2,1)} %bitcast.31), calls=%async_computation.6 | async-start | bytes 1048576 | tf_op jit(solution)/shard_map/all_to_all | solution.py:130
Sparse Core Ops, SparseCore 0:
  61.4 243.6 all-gather.4
  307.9 229.6 all-gather.6
  541.7 116.4 reduce-scatter.3
